TPU v7x, 256 devices: a whole 4x4x8 slice. The times are simulated.
256 devices in a mesh: seq: 128 (over y, z, x), head: 2 (over core).
Axes of the slice: x: 4, y: 4, z: 8, core: 2. Of those that a mesh axis runs over, the one named last changes fastest.
Arguments:
- queries: bfloat16 [8192, 1536], P('seq', 'head'), may hold values from -6 to 6
- key_vectors: bfloat16 [8192, 512], P('seq', 'head'), may hold values from -6 to 6
- value_vectors: bfloat16 [8192, 512], P('seq', 'head'), may hold values from -6 to 6
- lengths: int32 [64], replicated, may hold values from 1 to 256, 8192 in all
- out_weight: bfloat16 [1536, 1536], P('head', 'seq'), may hold values from -0.15625 to 0.15625
- residual: bfloat16 [8192, 1536], P(('seq', 'head')), may hold values from -6 to 6
- norm_gain: float32 [1536], replicated, may hold values from 0.1 to 1.9
- route_ids: int32 [8192, 6], P(('seq', 'head')), may hold values from 0 to 63, all different within a row; in each aligned block of 32 rows (0 to 31, 32 to 63, ...) at most 6 rows name the same one
- route_logits: float32 [8192, 6], P(('seq', 'head')), may hold values from -8 to 340
- shared_gate_up: bfloat16 [1536, 2, 1024], P(None, None, ('seq', 'head')), may hold values from -0.15625 to 0.15625
- shared_down: bfloat16 [1024, 1536], P(('seq', 'head')), may hold values from -0.1875 to 0.1875
- expert_gate_up: bfloat16 [128, 1536, 2, 256], P('seq'), may hold values from -0.15625 to 0.15625
- expert_down: bfloat16 [128, 256, 1536], P('seq'), may hold values from -0.25 to 0.25
- cache_blocks: bfloat16 [128, 128, 8, 4, 128], P('seq', None, None, 'head'), may hold values from -6 to 6
- block_table: int32 [128], replicated, may hold values from 0 to 127, each once
Outputs:
- layer_out: bfloat16 [8192, 1536], P(('seq', 'head'))
- cache_out: bfloat16 [128, 128, 8, 4, 128], P(None, 'seq', None, 'head')
Inputs may be any that keep to these rules, and one draw needn't show every extreme that they name: The lengths sum to 8192. `route_ids`: each token names 6 different experts; among the tokens of one device no expert is named more than 6 times. `block_table`: every block appears once.
All inputs are finite; a program needn't handle non-finite values.
Results may differ from a plain program's by a relative error of at most 0.0095.
Values may be sent and summed in bfloat16 or wider, within the bound.
A program may use at most 64 MiB of HBM per device.

v0:
```python
import math
import jax
import jax.numpy as jnp
from jax import lax
from jax.sharding import PartitionSpec as P

HD = 128
EXPERTS = 64
TOP = 6
REACH = 4
HALVES = 128
CAP = 6
NEGATIVE = -1e30
EPSILON = 1e-05


def from_behind(shard, axis, by):
    devices = lax.axis_size(axis)
    pairs = [(i, i + by) for i in range(devices) if 0 <= i + by < devices]
    return lax.ppermute(shard, axis, pairs)


def segment_of(positions, lengths):
    request_ends = jnp.cumsum(lengths)
    passed = (request_ends[None, :] <= positions[:, None]).astype(jnp.int32)
    return jnp.sum(passed, axis=1)


def shared_ffn(rows_in, gate_up_part, down_part):
    shared_both = jnp.einsum(
        "td,dcf->tcf", rows_in, gate_up_part, preferred_element_type=jnp.float32
    )
    shared_act = (jax.nn.silu(shared_both[:, 0]) * shared_both[:, 1]).astype(jnp.bfloat16)
    return jnp.dot(shared_act, down_part, preferred_element_type=jnp.float32)


def shards(
    queries,
    key_vectors,
    value_vectors,
    lengths,
    out_weight,
    residual,
    norm_gain,
    route_ids,
    route_logits,
    shared_gate_up,
    shared_down,
    expert_gate_up,
    expert_down,
    cache_blocks,
    block_table,
):
    handed = lax.all_to_all(cache_blocks, "seq", split_axis=1, concat_axis=0, tiled=True)
    cache_out = jnp.take(handed, block_table, axis=0)
    tok_rows = queries.shape[0]
    seq_index = lax.axis_index("seq")
    earlier = [
        from_behind((key_vectors, value_vectors), "seq", offset) for offset in range(REACH, 0, -1)
    ]
    window_keys = jnp.concatenate([member[0] for member in earlier] + [key_vectors], axis=0)
    window_values = jnp.concatenate([member[1] for member in earlier] + [value_vectors], axis=0)
    key_count = window_keys.shape[0]
    kv_heads = key_vectors.shape[1] // HD
    query_heads = queries.shape[1] // HD
    group_size = query_heads // kv_heads
    query_pos = seq_index * tok_rows + jnp.arange(tok_rows, dtype=jnp.int32)
    key_pos = (seq_index - REACH) * tok_rows + jnp.arange(key_count, dtype=jnp.int32)
    visible = (key_pos[None, :] >= 0) & (key_pos[None, :] <= query_pos[:, None])
    visible = visible & (
        segment_of(key_pos, lengths)[None, :] == segment_of(query_pos, lengths)[:, None]
    )
    query_part = queries.reshape(tok_rows, kv_heads, group_size, HD)
    key_part = window_keys.reshape(key_count, kv_heads, HD)
    value_part = window_values.reshape(key_count, kv_heads, HD)
    scores = jnp.einsum(
        "tkgd,wkd->kgtw", query_part, key_part, preferred_element_type=jnp.float32
    ) * (1.0 / math.sqrt(HD))
    scores = jnp.where(visible[None, None], scores, NEGATIVE)
    row_max = jnp.max(scores, axis=-1, keepdims=True)
    weights = jnp.exp(scores - row_max)
    row_total = jnp.sum(weights, axis=-1)
    weighted = jnp.einsum(
        "kgtw,wkd->tkgd",
        weights.astype(jnp.bfloat16),
        value_part,
        preferred_element_type=jnp.float32,
    )
    heads = (weighted / jnp.transpose(row_total, (2, 0, 1))[..., None]).astype(jnp.bfloat16)
    heads = heads.reshape(tok_rows, query_heads * HD)
    partial_out = jnp.dot(
        heads,
        lax.all_gather(out_weight, "seq", axis=1, tiled=True),
        preferred_element_type=jnp.float32,
    )
    attn_out = lax.psum_scatter(partial_out, "head", scatter_dimension=0, tiled=True)
    mixed = residual.astype(jnp.float32) + attn_out
    mean_square = jnp.mean(mixed * mixed, axis=-1, keepdims=True)
    normed = (mixed * lax.rsqrt(mean_square + EPSILON) * norm_gain).astype(jnp.bfloat16)
    gate_up_all, down_all = (
        lax.all_gather(shared_gate_up, ("seq", "head"), axis=2, tiled=True),
        lax.all_gather(shared_down, ("seq", "head"), axis=0, tiled=True),
    )
    shared_part = shared_ffn(normed, gate_up_all, down_all)
    own_tokens = normed.shape[0]
    width_model = normed.shape[1]
    flat_ids = route_ids.reshape(-1)
    onehot = (flat_ids[:, None] == jnp.arange(EXPERTS, dtype=jnp.int32)[None, :]).astype(jnp.int32)
    slot_rank = jnp.sum((jnp.cumsum(onehot, axis=0) - 1) * onehot, axis=1)
    first_slot = flat_ids * CAP + slot_rank
    second_slot = (flat_ids + EXPERTS) * CAP + slot_rank
    token_of = jnp.arange(flat_ids.shape[0], dtype=jnp.int32) // TOP
    routed_rows = normed[token_of]
    outgoing = jnp.zeros((HALVES * CAP, width_model), jnp.bfloat16)
    outgoing = outgoing.at[jnp.concatenate([first_slot, second_slot])].set(
        jnp.concatenate([routed_rows, routed_rows], axis=0)
    )
    local_halves = expert_gate_up.shape[0]
    outgoing = outgoing.reshape(HALVES // local_halves, local_halves, CAP, width_model)
    gate_up = jnp.einsum(
        "nsjd,sdcf->nsjcf",
        lax.all_to_all(outgoing, "seq", split_axis=0, concat_axis=0, tiled=True),
        expert_gate_up,
        preferred_element_type=jnp.float32,
    )
    expert_act = (jax.nn.silu(gate_up[:, :, :, 0]) * gate_up[:, :, :, 1]).astype(jnp.bfloat16)
    half_out = jnp.einsum(
        "nsjf,sfd->nsjd", expert_act, expert_down, preferred_element_type=jnp.float32
    ).astype(jnp.bfloat16)
    returned = lax.all_to_all(half_out, "seq", split_axis=0, concat_axis=0, tiled=True)
    returned = returned.reshape(HALVES * CAP, width_model)
    pair_sum = returned[first_slot].astype(jnp.float32) + returned[second_slot].astype(jnp.float32)
    route_probs = jax.nn.softmax(route_logits, axis=-1)
    routed = jnp.sum(
        route_probs[:, :, None] * pair_sum.reshape(own_tokens, TOP, width_model), axis=1
    )
    layer_out = (mixed + shared_part + routed).astype(jnp.bfloat16)
    return (layer_out, cache_out)


def solution(mesh):
    in_specs = (
        P("seq", "head"),
        P("seq", "head"),
        P("seq", "head"),
        P(),
        P("head", "seq"),
        P(("seq", "head"), None),
        P(),
        P(("seq", "head"), None),
        P(("seq", "head"), None),
        P(None, None, ("seq", "head")),
        P(("seq", "head"), None),
        P("seq", None, None, None),
        P("seq", None, None),
        P("seq", None, None, "head", None),
        P(),
    )
    out_specs = (P(("seq", "head"), None), P(None, "seq", None, "head", None))
    return jax.shard_map(shards, mesh=mesh, in_specs=in_specs, out_specs=out_specs, check_vma=False)
```

profile of v0, /device:TPU:1, one launch (start us, length us, event | category | flops | bytes accessed | tf_op | source)
XLA Modules:
  0.0 410.7 jit_solution(4338545764262982124)
XLA Ops:
  8.1 0.7 all-gather.8.cloned.1.call-update
  8.8 4.4 %collective-permute-start.4 = (bf16[64,256]{1,0:T(8,128)(2,1)}, bf16[64,256]{1,0:T(8,128)(2,1)S(1)}, u32[]{:S(2)}, u32[]{:S(2)}) collective-permute-start(bf16[64,256]{1,0:T(8,128)(2,1)} %param.16), channel_id=1, source_target_pairs={{0,8},{2,10},{4,12},{6,14},{8,16},{10,18},{12,20},{14,22},{16,24},... | collective-permute-start | bytes 98312 | tf_op jit(solution)/shard_map/ppermute | solution.py:20
  13.2 4.4 %collective-permute-start.5 = (bf16[64,256]{1,0:T(8,128)(2,1)}, bf16[64,256]{1,0:T(8,128)(2,1)S(1)}, u32[]{:S(2)}, u32[]{:S(2)}) collective-permute-start(bf16[64,256]{1,0:T(8,128)(2,1)} %param.16), channel_id=1, source_target_pairs={{0,6},{2,8},{4,10},{6,12},{8,14},{10,16},{12,18},{14,20},{16,22},{... | collective-permute-start | bytes 98312 | tf_op jit(solution)/shard_map/ppermute | solution.py:20
  17.6 3.8 collective-permute-start.6
  21.4 2.5 collective-permute-start.7
  23.9 3.6 collective-permute-start
  27.4 0.7 copy.54
  28.2 0.1 reduce-window.18
  28.3 0.1 reduce
  28.4 0.2 convert_reduce_fusion.1
  28.6 0.1 convert_reduce_fusion
  28.7 0.1 compare_and_fusion
  28.8 0.9 reshape.398
  29.8 6.5 %collective-permute-start.1 = (bf16[64,256]{1,0:T(8,128)(2,1)}, bf16[64,256]{1,0:T(8,128)(2,1)S(1)}, u32[]{:S(2)}, u32[]{:S(2)}) collective-permute-start(bf16[64,256]{1,0:T(8,128)(2,1)} %param.17), channel_id=1, source_target_pairs={{0,6},{2,8},{4,10},{6,12},{8,14},{10,16},{12,18},{14,20},{16,22},{... | collective-permute-start | bytes 98312 | tf_op jit(solution)/shard_map/ppermute | solution.py:20
  36.4 3.1 collective-permute-start.2
  39.5 1.4 collective-permute-start.3
  40.9 0.8 constant_dynamic-update-slice_fusion.5
  41.8 0.4 collective-permute-done.3
  42.2 0.8 constant_dynamic-update-slice_fusion
  43.0 0.3 fusion.48
  43.4 0.2 fusion.27
  43.6 0.3 fusion.23
  43.9 0.1 copy.58
  44.1 83.4 %all-gather.8.cloned.1.call-done = bf16[128,12,768]{2,1,0:T(8,128)(2,1)} async-done(((bf16[1,12,768]{2,1,0:T(8,128)(2,1)}), bf16[128,12,768]{2,1,0:T(8,128)(2,1)}) %all-gather.8.cloned.1.call-update) | async-done | bytes 2359312 | tf_op jit(solution)/shard_map/all_gather | solution.py:93
  127.5 3.6 reshape.454
  131.2 1.6 fusion.49
  132.8 0.5 all-gather.10.cloned.1.call-update
  133.4 0.6 copy.59
  134.1 0.1 copy.62
  134.2 0.1 reshape.400
  134.3 0.6 reduce-window.19
  134.9 0.2 slice_reduce_fusion
  135.2 0.1 bitcast_bitcast_fusion
  135.3 0.1 fusion.45
  135.4 12.7 %reduce-scatter.2.cloned.1.call-done = f32[32,1536]{1,0:T(8,128)} async-done(((f32[64,1536]{1,0:T(8,128)}), f32[32,1536]{1,0:T(8,128)}) %reduce-scatter.2.cloned.1.call-update) | async-done | bytes 196624 | tf_op jit(solution)/shard_map/reduce_scatter | solution.py:96
  148.1 1.1 multiply_reduce_fusion.1
  149.2 1.0 multiply_convert_fusion
  150.2 1.9 gather_fusion
  152.1 3.9 scatter_custom_fusion
  156.0 2.5 reshape.403
  158.5 89.1 %all_to_all.22 = bf16[128,1,6,1536]{3,2,1,0:T(8,128)(2,1)} all-to-all(bf16[128,1,6,1536]{3,2,1,0:T(8,128)(2,1)} %bitcast.96), channel_id=1, replica_groups=mesh['seq'=128,'head'=2] {'seq'}, dimensions={0} | all-to-all | bytes 4718592 | tf_op jit(solution)/shard_map/all_to_all | solution.py:122
  247.6 10.7 %all-to-all-start.2 = ((bf16[1,128,8,2,128]{4,3,2,0,1:T(2,128)(2,1)}), bf16[1,128,8,2,128]{4,3,2,0,1:T(2,128)(2,1)S(1)}, u32[]{:S(2)}, u32[]{:S(2)}) async-start(bf16[1,128,8,2,128]{4,3,2,0,1:T(2,128)(2,1)} %bitcast.36), calls=%async_computation.3 | async-start | bytes 1048576 | tf_op jit(solution)/shard_map/all_to_all | solution.py:54
  258.3 3.3 fusion.10
  261.6 0.8 fusion.2
  262.4 3.0 copy.68
  265.3 9.3 %all-to-all-done.2 = bf16[1,128,8,2,128]{4,3,2,0,1:T(2,128)(2,1)S(1)} async-done(((bf16[1,128,8,2,128]{4,3,2,0,1:T(2,128)(2,1)}), bf16[1,128,8,2,128]{4,3,2,0,1:T(2,128)(2,1)S(1)}, u32[]{:S(2)}, u32[]{:S(2)}) %all-to-all-start.2) | async-done | bytes 524320 | tf_op jit(solution)/shard_map/all_to_all | solution.py:54
  274.6 8.9 %all-to-all-start.1 = ((bf16[128,1,6,1536]{3,2,1,0:T(8,128)(2,1)}), bf16[128,1,6,1536]{3,2,1,0:T(8,128)(2,1)}, u32[]{:S(2)}, u32[]{:S(2)}) async-start(bf16[128,1,6,1536]{3,2,1,0:T(8,128)(2,1)} %copy.68), calls=%async_computation.2 | async-start | bytes 6291456 | tf_op jit(solution)/shard_map/all_to_all | solution.py:130
  283.6 0.1 copy.69
  283.7 0.1 mul.140
  283.8 0.1 copy.70
  283.9 0.1 mul.142
  284.0 0.1 copy.61
  284.2 1.6 gather_fusion.3
  285.8 1.4 fusion.26
  287.2 5.9 %reshape.456 = bf16[1024,1536]{1,0:T(8,128)(2,1)} reshape(bf16[256,4,1536]{2,1,0:T(4,128)(2,1)} %all-gather.10.cloned.1.call-done) | data formatting | bytes 6291456
  293.1 91.6 %all-gather.6.cloned.1.call-done = bf16[1536,2,1024]{0,1,2:T(2,128)(2,1)} async-done(((bf16[1536,2,4]{0,1,2:T(2,128)(2,1)}), bf16[1536,2,1024]{0,1,2:T(2,128)(2,1)}) %all-gather.6.cloned.1.call-update) | async-done | bytes 6291472 | tf_op jit(solution)/shard_map/all_gather | solution.py:101
  384.8 5.5 %fusion = f32[32,2,1024]{2,0,1:T(8,128)} fusion(bf16[1536,2,1024]{0,1,2:T(2,128)(2,1)} %all-gather.6.cloned.1.call-done, bf16[32,1536]{1,0:T(8,128)(2,1)S(1)} %multiply_convert_fusion), kind=kOutput, calls=%fused_computation.5 | convolution fusion | flops 201326592 | bytes 6651904 | tf_op jit(solution)/shard_map/td,dcf->tcf/dot_general | solution.py:30
  390.2 3.7 reshape.407
  393.9 1.9 gather_fusion.1
  395.8 1.9 gather_fusion.2
  397.7 1.4 convert_add_fusion
  399.1 0.2 add.235
  399.3 0.6 multiply_reduce_fusion
  399.8 3.4 fusion.7
  (63 shorter events, 0.7 us)
Async XLA Ops:
  8.0 253.6 %copy-start = (bf16[1,256,1536]{2,1,0:T(8,128)(2,1)S(1)}, bf16[1,256,1536]{2,1,0:T(8,128)(2,1)}, u32[]{:S(2)}) copy-start(bf16[1,256,1536]{2,1,0:T(8,128)(2,1)} %param.27) | copy-start | bytes 2359300
  8.0 119.5 %all-gather.8.cloned.1.call-start = ((), (), s32[]{:S(2)}) async-start(), calls=%async_computation.6 | async-start | bytes 3170304 | tf_op jit(solution)/shard_map/all_gather | solution.py:93
  8.7 139.4 %reduce-scatter.2.cloned.1.call-start = ((), (), s32[]{:S(2)}) async-start(), calls=%async_computation.4 | async-start | bytes 589824 | tf_op jit(solution)/shard_map/reduce_scatter | solution.py:96
  8.8 21.0 %collective-permute-start.4 = (bf16[64,256]{1,0:T(8,128)(2,1)}, bf16[64,256]{1,0:T(8,128)(2,1)S(1)}, u32[]{:S(2)}, u32[]{:S(2)}) collective-permute-start(bf16[64,256]{1,0:T(8,128)(2,1)} %param.16), channel_id=1, source_target_pairs={{0,8},{2,10},{4,12},{6,14},{8,16},{10,18},{12,20},{14,22},{16,24},... | collective-permute-start | bytes 98312 | tf_op jit(solution)/shard_map/ppermute | solution.py:20
  13.2 23.2 %collective-permute-start.5 = (bf16[64,256]{1,0:T(8,128)(2,1)}, bf16[64,256]{1,0:T(8,128)(2,1)S(1)}, u32[]{:S(2)}, u32[]{:S(2)}) collective-permute-start(bf16[64,256]{1,0:T(8,128)(2,1)} %param.16), channel_id=1, source_target_pairs={{0,6},{2,8},{4,10},{6,12},{8,14},{10,16},{12,18},{14,20},{16,22},{... | collective-permute-start | bytes 98312 | tf_op jit(solution)/shard_map/ppermute | solution.py:20
  17.6 22.0 %collective-permute-start.6 = (bf16[64,256]{1,0:T(8,128)(2,1)}, bf16[64,256]{1,0:T(8,128)(2,1)S(1)}, u32[]{:S(2)}, u32[]{:S(2)}) collective-permute-start(bf16[64,256]{1,0:T(8,128)(2,1)} %param.16), channel_id=1, source_target_pairs={{0,4},{2,6},{4,8},{6,10},{8,12},{10,14},{12,16},{14,18},{16,20},{1... | collective-permute-start | bytes 98312 | tf_op jit(solution)/shard_map/ppermute | solution.py:20
  21.4 19.5 %collective-permute-start.7 = (bf16[64,256]{1,0:T(8,128)(2,1)}, bf16[64,256]{1,0:T(8,128)(2,1)S(1)}, u32[]{:S(2)}, u32[]{:S(2)}) collective-permute-start(bf16[64,256]{1,0:T(8,128)(2,1)} %param.16), channel_id=1, source_target_pairs={{0,2},{2,4},{4,6},{6,8},{8,10},{10,12},{12,14},{14,16},{16,18},{18... | collective-permute-start | bytes 98312 | tf_op jit(solution)/shard_map/ppermute | solution.py:20
  23.9 17.8 %collective-permute-start = (bf16[64,256]{1,0:T(8,128)(2,1)}, bf16[64,256]{1,0:T(8,128)(2,1)S(1)}, u32[]{:S(2)}, u32[]{:S(2)}) collective-permute-start(bf16[64,256]{1,0:T(8,128)(2,1)} %param.17), channel_id=1, source_target_pairs={{0,8},{2,10},{4,12},{6,14},{8,16},{10,18},{12,20},{14,22},{16,24},... | collective-permute-start | bytes 98312 | tf_op jit(solution)/shard_map/ppermute | solution.py:20
  29.8 11.9 %collective-permute-start.1 = (bf16[64,256]{1,0:T(8,128)(2,1)}, bf16[64,256]{1,0:T(8,128)(2,1)S(1)}, u32[]{:S(2)}, u32[]{:S(2)}) collective-permute-start(bf16[64,256]{1,0:T(8,128)(2,1)} %param.17), channel_id=1, source_target_pairs={{0,6},{2,8},{4,10},{6,12},{8,14},{10,16},{12,18},{14,20},{16,22},{... | collective-permute-start | bytes 98312 | tf_op jit(solution)/shard_map/ppermute | solution.py:20
  36.4 5.4 %collective-permute-start.2 = (bf16[64,256]{1,0:T(8,128)(2,1)}, bf16[64,256]{1,0:T(8,128)(2,1)S(1)}, u32[]{:S(2)}, u32[]{:S(2)}) collective-permute-start(bf16[64,256]{1,0:T(8,128)(2,1)} %param.17), channel_id=1, source_target_pairs={{0,4},{2,6},{4,8},{6,10},{8,12},{10,14},{12,16},{14,18},{16,20},{1... | collective-permute-start | bytes 98312 | tf_op jit(solution)/shard_map/ppermute | solution.py:20
  39.5 2.7 collective-permute-start.3
  131.1 2.3 copy-start.3
  131.1 2.9 copy-start.4
  131.2 16.9 %copy-start.1 = (bf16[32,1536]{1,0:T(8,128)(2,1)S(1)}, bf16[32,1536]{1,0:T(8,128)(2,1)}, u32[]{:S(2)}) copy-start(bf16[32,1536]{1,0:T(8,128)(2,1)} %param.20) | copy-start | bytes 294916
  131.2 18.0 %copy-start.5 = (f32[1536]{0:T(1024)S(1)}, f32[1536]{0:T(1024)}, u32[]{:S(2)}) copy-start(f32[1536]{0:T(1024)} %param.21) | copy-start | bytes 18436
  132.8 154.4 %all-gather.10.cloned.1.call-start = ((), (), s32[]{:S(2)}) async-start(), calls=%async_computation.7 | async-start | bytes 3158016 | tf_op jit(solution)/shard_map/all_gather | solution.py:102
  133.4 251.4 %all-gather.6.cloned.1.call-start = ((), (), s32[]{:S(2)}) async-start(), calls=%async_computation.5 | async-start | bytes 6316032 | tf_op jit(solution)/shard_map/all_gather | solution.py:101
  158.5 99.8 %copy-start.6 = (bf16[1,1536,2,256]{3,2,1,0:T(2,128)(2,1)S(1)}, bf16[1,1536,2,256]{3,2,1,0:T(2,128)(2,1)}, u32[]{:S(2)}) copy-start(bf16[1,1536,2,256]{3,2,1,0:T(2,128)(2,1)} %param.26) | copy-start | bytes 4718596
  247.6 27.1 %all-to-all-start.2 = ((bf16[1,128,8,2,128]{4,3,2,0,1:T(2,128)(2,1)}), bf16[1,128,8,2,128]{4,3,2,0,1:T(2,128)(2,1)S(1)}, u32[]{:S(2)}, u32[]{:S(2)}) async-start(bf16[1,128,8,2,128]{4,3,2,0,1:T(2,128)(2,1)} %bitcast.36), calls=%async_computation.3 | async-start | bytes 1048576 | tf_op jit(solution)/shard_map/all_to_all | solution.py:54
  265.3 18.6 %copy-start.2 = (f32[32,6]{0,1:T(8,128)S(1)}, f32[32,6]{0,1:T(8,128)}, u32[]{:S(2)}) copy-start(f32[32,6]{0,1:T(8,128)} %param.23) | copy-start | bytes 2308
  265.3 18.8 %copy-start.7 = (s32[128]{0:T(128)S(1)}, s32[128]{0:T(128)}, u32[]{:S(2)}) copy-start(s32[128]{0:T(128)} %param.29) | copy-start | bytes 1540
  274.6 115.6 %all-to-all-start.1 = ((bf16[128,1,6,1536]{3,2,1,0:T(8,128)(2,1)}), bf16[128,1,6,1536]{3,2,1,0:T(8,128)(2,1)}, u32[]{:S(2)}, u32[]{:S(2)}) async-start(bf16[128,1,6,1536]{3,2,1,0:T(8,128)(2,1)} %copy.68), calls=%async_computation.2 | async-start | bytes 6291456 | tf_op jit(solution)/shard_map/all_to_all | solution.py:130
Sparse Core Ops, SparseCore 0:
  12.5 114.9 all-gather.7
  132.9 15.1 reduce-scatter.1
Sparse Core Ops, SparseCore 1:
  137.6 121.0 all-gather.9
  263.6 121.1 all-gather.5
where the time goes:
time: 412 us; the launch traced here: 411 us
  waiting for transfers between devices  199 us (48%)
  blocking collectives  89.1 us (22%)
  starting transfers between devices  49.4 us (12%)
  local copies, waits for them, and re-layouts  31.2 us (8%)
  between operations  16 us (4%)
  matrix products  15.2 us (4%)
  other arithmetic  11.1 us (3%)
    all_gather x1, waiting for transfers between devices, shards(): lax.all_gather(shared_gate_up, ('seq', 'head'), axis=2, tiled=True)  91.6 us
    all_to_all x1, blocking collectives, shards(): lax.all_to_all(outgoing, 'seq', split_axis=0, concat_axis=0, tiled=True)  89.1 us
    all_gather x1, waiting for transfers between devices, shards(): lax.all_gather(out_weight, 'seq', axis=1, tiled=True)  83.4 us
    ppermute x8, starting transfers between devices, from_behind(): return lax.ppermute(shard, axis, pairs)  29.7 us
    reduce_scatter x1, waiting for transfers between devices, shards(): lax.psum_scatter(partial_out, 'head', scatter_dimension=0, tiled=True)  12.7 us
    all_to_all x1, starting transfers between devices, shards(): lax.all_to_all(cache_blocks, 'seq', split_axis=1, concat_axis=0, tiled=True)  10.7 us
    unnamed x28, local copies, waits for them, and re-layouts  10.3 us
    all_to_all x1, waiting for transfers between devices, shards(): lax.all_to_all(cache_blocks, 'seq', split_axis=1, concat_axis=0, tiled=True)  9.29 us
  transfers between devices with their start and end apart: 14, of which 5 were waited for; matrix products, arithmetic and copies ran while one was open for 10% of the time, Pallas kernels for 0%

commit v1 on v0

--- a/solution.py
+++ b/solution.py
@@ -90,7 +90,9 @@
     heads = heads.reshape(tok_rows, query_heads * HD)
     partial_out = jnp.dot(
         heads,
-        lax.all_gather(out_weight, "seq", axis=1, tiled=True),
+        jnp.concatenate(
+            lax.all_to_all(jnp.stack([out_weight] * lax.axis_size("seq")), "seq", 0, 0), axis=1
+        ),
         preferred_element_type=jnp.float32,
     )
     attn_out = lax.psum_scatter(partial_out, "head", scatter_dimension=0, tiled=True)

time: 412 us -> 397 us (0.964)
  waiting for transfers between devices: 199 us -> 170 us
  starting transfers between devices: 49.4 us -> 63.4 us
    all_gather x1 -> x0, waiting for transfers between devices: 83.4 us -> none  [shards(): lax.all_gather(out_weight, 'seq', axis=1, tiled=True)]
    ppermute x8, waiting for transfers between devices: 0.44 us -> 48.7 us  [from_behind(): return lax.ppermute(shard, axis, pairs)]
    all_to_all x0 -> x1, starting transfers between devices: none -> 16.9 us  [shards(): lax.all_to_all(jnp.stack([out_weight] * lax.axis_size('seq')), 'seq', 0, 0)]
    reduce_scatter x1, waiting for transfers between devices: 12.7 us -> 19.6 us  [shards(): lax.psum_scatter(partial_out, 'head', scatter_dimension=0, tiled=True)]
    unnamed x28 -> x35, local copies, waits for them, and re-layouts: 10.3 us -> 6.72 us
  transfers between devices with their start and end apart: 14 -> 14, of which waited for: 5 -> 5; matrix products, arithmetic and copies ran while one was open for 10% -> 9% of each run, Pallas kernels for 0% -> 0%
where the time goes in v1:
time: 397 us; the launch traced here: 395 us
  waiting for transfers between devices  170 us (43%)
  blocking collectives  89.1 us (22%)
  starting transfers between devices  63.4 us (16%)
  local copies, waits for them, and re-layouts  30.8 us (8%)
  between operations  16.1 us (4%)
  matrix products  15.2 us (4%)
  other arithmetic  11.1 us (3%)
    all_gather x1, waiting for transfers between devices, shards(): lax.all_gather(shared_gate_up, ('seq', 'head'), axis=2, tiled=True)  91.3 us
    all_to_all x1, blocking collectives, shards(): lax.all_to_all(outgoing, 'seq', split_axis=0, concat_axis=0, tiled=True)  89.1 us
    ppermute x8, waiting for transfers between devices, from_behind(): return lax.ppermute(shard, axis, pairs)  48.7 us
    ppermute x8, starting transfers between devices, from_behind(): return lax.ppermute(shard, axis, pairs)  26.5 us
    reduce_scatter x1, waiting for transfers between devices, shards(): lax.psum_scatter(partial_out, 'head', scatter_dimension=0, tiled=True)  19.6 us
    all_to_all x1, starting transfers between devices, shards(): lax.all_to_all(jnp.stack([out_weight] * lax.axis_size('seq')), 'seq', 0, 0)  16.9 us
    all_to_all x1, starting transfers between devices, shards(): lax.all_to_all(cache_blocks, 'seq', split_axis=1, concat_axis=0, tiled=True)  10.7 us
    all_to_all x1, waiting for transfers between devices, shards(): lax.all_to_all(cache_blocks, 'seq', split_axis=1, concat_axis=0, tiled=True)  9.46 us
  transfers between devices with their start and end apart: 14, of which 5 were waited for; matrix products, arithmetic and copies ran while one was open for 9% of the time, Pallas kernels for 0%

profile of v1, /device:TPU:1, one launch (start us, length us, event | category | flops | bytes accessed | tf_op | source)
XLA Modules:
  0.0 395.4 jit_solution(853566011236471502)
XLA Ops:
  8.0 2.7 stack.2
  10.7 16.9 %all-to-all-start = ((bf16[128,768,12]{1,2,0:T(8,128)(2,1)}), bf16[128,768,12]{1,2,0:T(8,128)(2,1)}, u32[]{:S(2)}, u32[]{:S(2)}) async-start(bf16[128,768,12]{1,2,0:T(8,128)(2,1)} %stack.2), calls=%async_computation | async-start | bytes 6291456 | tf_op jit(solution)/shard_map/all_to_all | solution.py:94
  27.7 2.4 collective-permute-start.4
  30.2 4.3 %collective-permute-start.5 = (bf16[64,256]{1,0:T(8,128)(2,1)S(1)}, bf16[64,256]{1,0:T(8,128)(2,1)S(1)}, u32[]{:S(2)}, u32[]{:S(2)}) collective-permute-start(bf16[64,256]{1,0:T(8,128)(2,1)S(1)} %copy-done.4), channel_id=1, source_target_pairs={{0,6},{2,8},{4,10},{6,12},{8,14},{10,16},{12,18},{14,20},{16,22},{... | collective-permute-start | bytes 98312 | tf_op jit(solution)/shard_map/ppermute | solution.py:20
  34.5 3.4 collective-permute-start.6
  37.9 2.5 collective-permute-start.7
  40.4 3.1 collective-permute-start
  43.5 0.1 copy.55
  43.6 0.1 reduce-window.18
  43.7 0.1 reduce
  43.8 0.2 convert_reduce_fusion.1
  44.0 0.1 convert_reduce_fusion
  44.1 0.1 compare_and_fusion
  44.3 47.9 %collective-permute-done.4 = bf16[64,256]{1,0:T(8,128)(2,1)S(1)} collective-permute-done((bf16[64,256]{1,0:T(8,128)(2,1)S(1)}, bf16[64,256]{1,0:T(8,128)(2,1)S(1)}, u32[]{:S(2)}, u32[]{:S(2)}) %collective-permute-start.4) | collective-permute-done | bytes 32800 | tf_op jit(solution)/shard_map/ppermute | solution.py:20
  92.2 2.7 collective-permute-start.1
  94.9 5.7 %collective-permute-start.2 = (bf16[64,256]{1,0:T(8,128)(2,1)S(1)}, bf16[64,256]{1,0:T(8,128)(2,1)S(1)}, u32[]{:S(2)}, u32[]{:S(2)}) collective-permute-start(bf16[64,256]{1,0:T(8,128)(2,1)S(1)} %copy-done.5), channel_id=1, source_target_pairs={{0,4},{2,6},{4,8},{6,10},{8,12},{10,14},{12,16},{14,18},{16,20},{1... | collective-permute-start | bytes 98312 | tf_op jit(solution)/shard_map/ppermute | solution.py:20
  100.6 2.4 collective-permute-start.3
  103.2 0.8 collective-permute-done.3
  104.1 0.3 fusion.48
  104.5 0.2 fusion.27
  104.7 0.3 fusion.23
  105.0 0.1 copy.59
  105.1 0.1 reshape.407
  105.2 3.6 reshape.409
  108.9 1.6 fusion.49
  110.5 0.0 all-gather.6.cloned.1.call-start
  110.6 0.5 all-gather.6.cloned.1.call-update
  111.2 0.6 copy.60
  111.8 0.1 copy.63
  111.9 0.1 reshape.410
  112.0 0.6 reduce-window.19
  112.7 0.2 slice_reduce_fusion
  112.9 0.1 bitcast_bitcast_fusion
  113.0 0.1 fusion.45
  113.2 19.6 %reduce-scatter.2.cloned.1.call-done = f32[32,1536]{1,0:T(8,128)} async-done(((f32[64,1536]{1,0:T(8,128)}), f32[32,1536]{1,0:T(8,128)}) %reduce-scatter.2.cloned.1.call-update) | async-done | bytes 196624 | tf_op jit(solution)/shard_map/reduce_scatter | solution.py:98
  132.8 1.1 multiply_reduce_fusion.1
  133.9 1.0 multiply_convert_fusion
  134.9 1.9 gather_fusion
  136.8 3.9 scatter_custom_fusion
  140.7 2.5 reshape.413
  143.1 89.1 %all_to_all.27 = bf16[128,1,6,1536]{3,2,1,0:T(8,128)(2,1)} all-to-all(bf16[128,1,6,1536]{3,2,1,0:T(8,128)(2,1)} %bitcast.96), channel_id=1, replica_groups=mesh['seq'=128,'head'=2] {'seq'}, dimensions={0} | all-to-all | bytes 4718592 | tf_op jit(solution)/shard_map/all_to_all | solution.py:124
  232.2 10.7 %all-to-all-start.3 = ((bf16[1,128,8,2,128]{4,3,2,0,1:T(2,128)(2,1)}), bf16[1,128,8,2,128]{4,3,2,0,1:T(2,128)(2,1)S(1)}, u32[]{:S(2)}, u32[]{:S(2)}) async-start(bf16[1,128,8,2,128]{4,3,2,0,1:T(2,128)(2,1)} %bitcast.35), calls=%async_computation.4 | async-start | bytes 1048576 | tf_op jit(solution)/shard_map/all_to_all | solution.py:54
  242.9 3.3 fusion.10
  246.2 0.8 fusion.2
  247.0 3.0 copy.69
  250.0 9.5 %all-to-all-done.3 = bf16[1,128,8,2,128]{4,3,2,0,1:T(2,128)(2,1)S(1)} async-done(((bf16[1,128,8,2,128]{4,3,2,0,1:T(2,128)(2,1)}), bf16[1,128,8,2,128]{4,3,2,0,1:T(2,128)(2,1)S(1)}, u32[]{:S(2)}, u32[]{:S(2)}) %all-to-all-start.3) | async-done | bytes 524320 | tf_op jit(solution)/shard_map/all_to_all | solution.py:54
  259.5 9.1 %all-to-all-start.2 = ((bf16[128,1,6,1536]{3,2,1,0:T(8,128)(2,1)}), bf16[128,1,6,1536]{3,2,1,0:T(8,128)(2,1)}, u32[]{:S(2)}, u32[]{:S(2)}) async-start(bf16[128,1,6,1536]{3,2,1,0:T(8,128)(2,1)} %copy.69), calls=%async_computation.3 | async-start | bytes 6291456 | tf_op jit(solution)/shard_map/all_to_all | solution.py:132
  268.6 0.1 copy.70
  268.7 0.1 mul.140
  268.8 0.1 copy.71
  268.9 0.1 mul.142
  269.1 0.1 copy.62
  269.3 1.6 gather_fusion.3
  270.9 1.4 fusion.26
  272.3 5.9 %reshape.464 = bf16[1024,1536]{1,0:T(8,128)(2,1)} reshape(bf16[256,4,1536]{2,1,0:T(4,128)(2,1)} %all-gather.6.cloned.1.call-done) | data formatting | bytes 6291456
  278.2 91.3 %all-gather.4.cloned.1.call-done = bf16[1536,2,1024]{0,1,2:T(2,128)(2,1)} async-done(((bf16[1536,2,4]{0,1,2:T(2,128)(2,1)}), bf16[1536,2,1024]{0,1,2:T(2,128)(2,1)}) %all-gather.4.cloned.1.call-update) | async-done | bytes 6291472 | tf_op jit(solution)/shard_map/all_gather | solution.py:103
  369.5 5.5 %fusion = f32[32,2,1024]{2,0,1:T(8,128)} fusion(bf16[1536,2,1024]{0,1,2:T(2,128)(2,1)} %all-gather.4.cloned.1.call-done, bf16[32,1536]{1,0:T(8,128)(2,1)S(1)} %multiply_convert_fusion), kind=kOutput, calls=%fused_computation.5 | convolution fusion | flops 201326592 | bytes 6651904 | tf_op jit(solution)/shard_map/td,dcf->tcf/dot_general | solution.py:30
  375.0 3.7 reshape.417
  378.7 1.9 gather_fusion.1
  380.6 1.9 gather_fusion.2
  382.5 1.4 convert_add_fusion
  383.9 0.2 add.235
  384.0 0.6 multiply_reduce_fusion
  384.6 3.4 fusion.7
  (71 shorter events, 0.6 us)
Async XLA Ops:
  8.0 238.2 %copy-start = (bf16[1,256,1536]{2,1,0:T(8,128)(2,1)S(1)}, bf16[1,256,1536]{2,1,0:T(8,128)(2,1)}, u32[]{:S(2)}) copy-start(bf16[1,256,1536]{2,1,0:T(8,128)(2,1)} %param.27) | copy-start | bytes 2359300
  10.7 17.0 %copy-start.4 = (bf16[64,256]{1,0:T(8,128)(2,1)S(1)}, bf16[64,256]{1,0:T(8,128)(2,1)}, u32[]{:S(2)}) copy-start(bf16[64,256]{1,0:T(8,128)(2,1)} %param.16) | copy-start | bytes 98308
  10.7 29.6 %copy-start.5 = (bf16[64,256]{1,0:T(8,128)(2,1)S(1)}, bf16[64,256]{1,0:T(8,128)(2,1)}, u32[]{:S(2)}) copy-start(bf16[64,256]{1,0:T(8,128)(2,1)} %param.17) | copy-start | bytes 98308
  10.7 32.8 %copy-start.9 = (s32[64]{0:T(128)S(1)}, s32[64]{0:T(128)}, u32[]{:S(2)}) copy-start(s32[64]{0:T(128)} %param.18) | copy-start | bytes 772
  10.7 33.5 %copy-start.2 = (bf16[64,768]{1,0:T(8,128)(2,1)S(1)}, bf16[64,768]{1,0:T(8,128)(2,1)}, u32[]{:S(2)}) copy-start(bf16[64,768]{1,0:T(8,128)(2,1)} %param.15) | copy-start | bytes 294916
  10.7 94.5 %all-to-all-start = ((bf16[128,768,12]{1,2,0:T(8,128)(2,1)}), bf16[128,768,12]{1,2,0:T(8,128)(2,1)}, u32[]{:S(2)}, u32[]{:S(2)}) async-start(bf16[128,768,12]{1,2,0:T(8,128)(2,1)} %stack.2), calls=%async_computation | async-start | bytes 6291456 | tf_op jit(solution)/shard_map/all_to_all | solution.py:94
  27.7 105.1 %reduce-scatter.2.cloned.1.call-start = ((), (), s32[]{:S(2)}) async-start(), calls=%async_computation.5 | async-start | bytes 589824 | tf_op jit(solution)/shard_map/reduce_scatter | solution.py:98
  27.7 64.4 %collective-permute-start.4 = (bf16[64,256]{1,0:T(8,128)(2,1)S(1)}, bf16[64,256]{1,0:T(8,128)(2,1)S(1)}, u32[]{:S(2)}, u32[]{:S(2)}) collective-permute-start(bf16[64,256]{1,0:T(8,128)(2,1)S(1)} %copy-done.4), channel_id=1, source_target_pairs={{0,8},{2,10},{4,12},{6,14},{8,16},{10,18},{12,20},{14,22},{16,24},... | collective-permute-start | bytes 98312 | tf_op jit(solution)/shard_map/ppermute | solution.py:20
  30.2 64.7 %collective-permute-start.5 = (bf16[64,256]{1,0:T(8,128)(2,1)S(1)}, bf16[64,256]{1,0:T(8,128)(2,1)S(1)}, u32[]{:S(2)}, u32[]{:S(2)}) collective-permute-start(bf16[64,256]{1,0:T(8,128)(2,1)S(1)} %copy-done.4), channel_id=1, source_target_pairs={{0,6},{2,8},{4,10},{6,12},{8,14},{10,16},{12,18},{14,20},{16,22},{... | collective-permute-start | bytes 98312 | tf_op jit(solution)/shard_map/ppermute | solution.py:20
  34.5 66.2 %collective-permute-start.6 = (bf16[64,256]{1,0:T(8,128)(2,1)S(1)}, bf16[64,256]{1,0:T(8,128)(2,1)S(1)}, u32[]{:S(2)}, u32[]{:S(2)}) collective-permute-start(bf16[64,256]{1,0:T(8,128)(2,1)S(1)} %copy-done.4), channel_id=1, source_target_pairs={{0,4},{2,6},{4,8},{6,10},{8,12},{10,14},{12,16},{14,18},{16,20},{1... | collective-permute-start | bytes 98312 | tf_op jit(solution)/shard_map/ppermute | solution.py:20
  37.9 65.2 %collective-permute-start.7 = (bf16[64,256]{1,0:T(8,128)(2,1)S(1)}, bf16[64,256]{1,0:T(8,128)(2,1)S(1)}, u32[]{:S(2)}, u32[]{:S(2)}) collective-permute-start(bf16[64,256]{1,0:T(8,128)(2,1)S(1)} %copy-done.4), channel_id=1, source_target_pairs={{0,2},{2,4},{4,6},{6,8},{8,10},{10,12},{12,14},{14,16},{16,18},{18... | collective-permute-start | bytes 98312 | tf_op jit(solution)/shard_map/ppermute | solution.py:20
  40.4 62.7 %collective-permute-start = (bf16[64,256]{1,0:T(8,128)(2,1)S(1)}, bf16[64,256]{1,0:T(8,128)(2,1)S(1)}, u32[]{:S(2)}, u32[]{:S(2)}) collective-permute-start(bf16[64,256]{1,0:T(8,128)(2,1)S(1)} %copy-done.5), channel_id=1, source_target_pairs={{0,8},{2,10},{4,12},{6,14},{8,16},{10,18},{12,20},{14,22},{16,24},... | collective-permute-start | bytes 98312 | tf_op jit(solution)/shard_map/ppermute | solution.py:20
  92.2 11.0 %collective-permute-start.1 = (bf16[64,256]{1,0:T(8,128)(2,1)S(1)}, bf16[64,256]{1,0:T(8,128)(2,1)S(1)}, u32[]{:S(2)}, u32[]{:S(2)}) collective-permute-start(bf16[64,256]{1,0:T(8,128)(2,1)S(1)} %copy-done.5), channel_id=1, source_target_pairs={{0,6},{2,8},{4,10},{6,12},{8,14},{10,16},{12,18},{14,20},{16,22},{... | collective-permute-start | bytes 98312 | tf_op jit(solution)/shard_map/ppermute | solution.py:20
  94.9 8.3 %collective-permute-start.2 = (bf16[64,256]{1,0:T(8,128)(2,1)S(1)}, bf16[64,256]{1,0:T(8,128)(2,1)S(1)}, u32[]{:S(2)}, u32[]{:S(2)}) collective-permute-start(bf16[64,256]{1,0:T(8,128)(2,1)S(1)} %copy-done.5), channel_id=1, source_target_pairs={{0,4},{2,6},{4,8},{6,10},{8,12},{10,14},{12,16},{14,18},{16,20},{1... | collective-permute-start | bytes 98312 | tf_op jit(solution)/shard_map/ppermute | solution.py:20
  100.6 3.4 collective-permute-start.3
  108.9 2.3 copy-start.6
  108.9 2.9 copy-start.7
  108.9 23.9 %copy-start.1 = (bf16[32,1536]{1,0:T(8,128)(2,1)S(1)}, bf16[32,1536]{1,0:T(8,128)(2,1)}, u32[]{:S(2)}) copy-start(bf16[32,1536]{1,0:T(8,128)(2,1)} %param.20) | copy-start | bytes 294916
  108.9 25.0 %copy-start.8 = (f32[1536]{0:T(1024)S(1)}, f32[1536]{0:T(1024)}, u32[]{:S(2)}) copy-start(f32[1536]{0:T(1024)} %param.21) | copy-start | bytes 18436
  110.5 161.7 %all-gather.6.cloned.1.call-start = ((), (), s32[]{:S(2)}) async-start(), calls=%async_computation.7 | async-start | bytes 3158016 | tf_op jit(solution)/shard_map/all_gather | solution.py:104
  111.1 258.4 %all-gather.4.cloned.1.call-start = ((), (), s32[]{:S(2)}) async-start(), calls=%async_computation.6 | async-start | bytes 6316032 | tf_op jit(solution)/shard_map/all_gather | solution.py:103
  143.1 99.8 %copy-start.10 = (bf16[1,1536,2,256]{3,2,1,0:T(2,128)(2,1)S(1)}, bf16[1,1536,2,256]{3,2,1,0:T(2,128)(2,1)}, u32[]{:S(2)}) copy-start(bf16[1,1536,2,256]{3,2,1,0:T(2,128)(2,1)} %param.26) | copy-start | bytes 4718596
  232.2 27.2 %all-to-all-start.3 = ((bf16[1,128,8,2,128]{4,3,2,0,1:T(2,128)(2,1)}), bf16[1,128,8,2,128]{4,3,2,0,1:T(2,128)(2,1)S(1)}, u32[]{:S(2)}, u32[]{:S(2)}) async-start(bf16[1,128,8,2,128]{4,3,2,0,1:T(2,128)(2,1)} %bitcast.35), calls=%async_computation.4 | async-start | bytes 1048576 | tf_op jit(solution)/shard_map/all_to_all | solution.py:54
  250.0 19.0 %copy-start.3 = (f32[32,6]{0,1:T(8,128)S(1)}, f32[32,6]{0,1:T(8,128)}, u32[]{:S(2)}) copy-start(f32[32,6]{0,1:T(8,128)} %param.23) | copy-start | bytes 2308
  250.0 19.2 %copy-start.11 = (s32[128]{0:T(128)S(1)}, s32[128]{0:T(128)}, u32[]{:S(2)}) copy-start(s32[128]{0:T(128)} %param.29) | copy-start | bytes 1540
  259.5 115.5 %all-to-all-start.2 = ((bf16[128,1,6,1536]{3,2,1,0:T(8,128)(2,1)}), bf16[128,1,6,1536]{3,2,1,0:T(8,128)(2,1)}, u32[]{:S(2)}, u32[]{:S(2)}) async-start(bf16[128,1,6,1536]{3,2,1,0:T(8,128)(2,1)} %copy.69), calls=%async_computation.3 | async-start | bytes 6291456 | tf_op jit(solution)/shard_map/all_to_all | solution.py:132
Sparse Core Ops, SparseCore 0:
  110.6 22.0 reduce-scatter.1
Sparse Core Ops, SparseCore 1:
  115.3 127.9 all-gather.5
  248.2 121.2 all-gather.3
